TPU v7x, 32 devices: a whole 2x2x4 slice. The times are simulated.
32 devices in a mesh: dom: 8 (over y, x, core), rep: 4 (over z).
Axes of the slice: x: 2, y: 2, z: 4, core: 2. Of those that a mesh axis runs over, the one named last changes fastest.
Arguments:
- hop_feats: bfloat16 [3, 65536, 128], P(None, ('dom', 'rep')), may hold values from -6 to 6
- adj_local: bfloat16 [512, 12, 128, 128], P(('dom', 'rep')), may hold values from -0.125 to 0.125
- local_cols: int32 [512, 12], P(('dom', 'rep')), may hold values from 0 to 15
- adj_halo: bfloat16 [512, 4, 128, 128], P(('dom', 'rep')), may hold values from -0.125 to 0.125
- halo_cols: int32 [512, 4], P(('dom', 'rep')), may hold values from 0 to 3
- boundary_rows: int32 [32, 512], P(('dom', 'rep')), may hold values from 0 to 2047
- train_ids: int32 [32, 2048], P(('dom', 'rep')), may hold values from 0 to 2047, as said below
- shuffle: int32 [32, 2048], P(('dom', 'rep')), may hold values from 0 to 2047, as said below
- labels: int32 [65536], P(('dom', 'rep')), may hold values from 0 to 171
- labelled: int32 [65536], P(('dom', 'rep')), may hold values from 0 to 1
- w_first: bfloat16 [512, 1024], P(None, 'rep'), may hold values from -1 to 1
- w_second: bfloat16 [1024, 172], P('rep'), may hold values from -2 to 2
Outputs:
- next_hop: bfloat16 [65536, 128], P(('dom', 'rep'))
- batch_loss: float32 [32, 32], P(('dom', 'rep'))
- grad_first: float32 [512, 1024], P('dom', 'rep')
- grad_second: float32 [1024, 172], P('rep')
Inputs may be any that keep to these rules, and one draw needn't show every extreme that they name: `local_cols`: local tile indices of the partition's own row tiles. `halo_cols`: indices of received boundary tiles. `boundary_rows`: rows of the sending partition itself. `train_ids`: rows of the partition itself. `shuffle`: each row is a permutation of 0 .. 2047.
All inputs are finite; a program needn't handle non-finite values.
Results may differ from a plain program's by a relative error of at most 0.005.
The roundings to bfloat16 on the way count: a program that leaves them out, or rounds other values in their place, can miss the bound.
Values may be sent and summed in bfloat16 or wider, within the bound.
No kernel may reach another device: no remote copies, remote signals or barrier semaphores. Data moves between devices by JAX's collectives and lax.ppermute only.
A program may use at most 128 MiB of HBM per device.

v0:
```python
import jax
import jax.numpy as jnp
from jax import lax
from jax.sharding import PartitionSpec as P


def loss_head(logits, targets, weights_row):
    row_max = jnp.max(logits, axis=1, keepdims=True)
    expos = jnp.exp(logits - row_max)
    totals = jnp.sum(expos, axis=1, keepdims=True)
    classes = lax.broadcasted_iota(jnp.int32, logits.shape, 1)
    onehot = (classes == targets[:, None]).astype(jnp.float32)
    cross = jnp.log(totals[:, 0]) + row_max[:, 0] - jnp.sum(onehot * logits, axis=1)
    count = jnp.maximum(jnp.sum(weights_row), 1.0)
    dlogits = ((expos / totals - onehot) * (weights_row / count)[:, None]).astype(jnp.bfloat16)
    return (cross, dlogits)


def source_losses(cross, weights_row, groups):
    masks = weights_row.reshape(groups, -1)
    sums = jnp.sum(masks * cross.reshape(groups, -1), axis=1)
    return sums / jnp.maximum(jnp.sum(masks, axis=1), 1.0)


def batch_norm(pre):
    center = pre - jnp.mean(pre, axis=-2, keepdims=True)
    rstd = lax.rsqrt(jnp.mean(center * center, axis=-2, keepdims=True) + 1e-05)
    return (center * rstd, rstd)


def norm_back(grad, normed, rstd):
    mean_grad = jnp.mean(grad, axis=-2, keepdims=True)
    mean_proj = jnp.mean(grad * normed, axis=-2, keepdims=True)
    return (grad - mean_grad - normed * mean_proj) * rstd


def contract_rows(left, right):
    return lax.dot_general(
        left, right, (((0,), (0,)), ((), ())), preferred_element_type=jnp.float32
    )


def shards(
    hop_feats,
    adj_local,
    local_cols,
    adj_halo,
    halo_cols,
    boundary_rows,
    train_ids,
    shuffle,
    labels,
    labelled,
    w_first,
    w_second,
):
    num_dom = lax.axis_size("dom")
    num_rep = lax.axis_size("rep")
    devices = num_dom * num_rep
    tile = adj_local.shape[-1]
    row_tiles = adj_local.shape[0]
    rows = row_tiles * tile
    width = hop_feats.shape[2]
    hop_two = hop_feats[2]
    sent = jnp.take(hop_two, boundary_rows[0], axis=0)
    halo = lax.all_to_all(sent, ("dom", "rep"), split_axis=0, concat_axis=0, tiled=True)
    halo_count = halo.shape[0] // tile
    own_tiles = hop_two.reshape(row_tiles, tile, width)
    near = jnp.take(own_tiles, local_cols, axis=0)
    summed = jnp.einsum("ikab,ikbc->iac", adj_local, near, preferred_element_type=jnp.float32)
    far = jnp.take(halo.reshape(halo_count, tile, width), halo_cols, axis=0)
    summed = summed + jnp.einsum(
        "ikab,ikbc->iac", adj_halo, far, preferred_element_type=jnp.float32
    )
    next_hop = summed.reshape(rows, width).astype(jnp.bfloat16)
    order = jnp.take(train_ids[0], shuffle[0], axis=0)
    allfeat = jnp.concatenate([hop_feats[0], hop_feats[1], hop_two, next_hop], axis=1)
    feats = jnp.take(allfeat, order, axis=0)
    own_labels = jnp.take(labels, order, axis=0)
    own_marks = jnp.take(labelled, order, axis=0)
    target_pair = jnp.stack([own_labels, own_marks], axis=0)
    batch = lax.all_to_all(feats, ("dom", "rep"), split_axis=0, concat_axis=0, tiled=True)
    got_pair = lax.all_to_all(target_pair, ("dom", "rep"), split_axis=1, concat_axis=1, tiled=True)
    targets = got_pair[0]
    weights_row = got_pair[1].astype(jnp.float32)
    first_whole, second_whole = (
        lax.all_gather(w_first, "rep", axis=1, tiled=True),
        lax.all_gather(w_second, "rep", axis=0, tiled=True),
    )
    hidden_pre = jnp.dot(batch, first_whole, preferred_element_type=jnp.float32)
    normed, rstd = batch_norm(hidden_pre)
    hidden = jnp.maximum(normed, 0.0).astype(jnp.bfloat16)
    logits = jnp.dot(hidden, second_whole, preferred_element_type=jnp.float32)
    cross, dlogits = loss_head(logits, targets, weights_row)
    grad_two_full = contract_rows(hidden, dlogits)
    dhidden = lax.dot_general(
        dlogits, second_whole, (((1,), (1,)), ((), ())), preferred_element_type=jnp.float32
    )
    masked = jnp.where(normed > 0, dhidden, 0.0)
    dpre = norm_back(masked, normed, rstd).astype(jnp.bfloat16)
    grad_one_full = contract_rows(batch, dpre)
    grad_one_rep, grad_two_rep = (
        lax.psum_scatter(grad_one_full, "rep", scatter_dimension=1, tiled=True),
        lax.psum_scatter(grad_two_full, "rep", scatter_dimension=0, tiled=True),
    )
    grad_one = lax.psum_scatter(grad_one_rep, "dom", scatter_dimension=0, tiled=True)
    grad_two = lax.psum(grad_two_rep, "dom")
    loss = source_losses(cross, weights_row, devices)
    return (next_hop, loss.reshape(1, devices), grad_one, grad_two)


def solution(mesh):
    placed = (
        P(None, ("dom", "rep"), None),
        P(("dom", "rep"), None, None, None),
        P(("dom", "rep"), None),
        P(("dom", "rep"), None, None, None),
        P(("dom", "rep"), None),
        P(("dom", "rep"), None),
        P(("dom", "rep"), None),
        P(("dom", "rep"), None),
        P(("dom", "rep")),
        P(("dom", "rep")),
        P(None, "rep"),
        P("rep", None),
    )
    return jax.shard_map(
        shards,
        mesh=mesh,
        in_specs=placed,
        out_specs=(
            P(("dom", "rep"), None),
            P(("dom", "rep"), None),
            P("dom", "rep"),
            P("rep", None),
        ),
        check_vma=False,
    )
```

profile of v0, /device:TPU:0, one launch (start us, length us, event | category | flops | bytes accessed | tf_op | source)
XLA Modules:
  0.0 375.0 jit_solution(16362593156664925678)
XLA Ops:
  7.2 0.8 compare_select_fusion.5
  8.0 0.5 broadcast.147
  8.5 1.3 reduce.13
  10.0 2.6 slice_bitcast_fusion.1
  12.7 1.3 gather_fusion.1
  14.0 0.8 broadcast_select_fusion.1
  14.8 7.3 %all-to-all-start = ((bf16[32,16,128]{2,1,0:T(8,128)(2,1)}), bf16[32,16,128]{2,1,0:T(8,128)(2,1)S(1)}, u32[]{:S(2)}, u32[]{:S(2)}) async-start(bf16[32,16,128]{2,1,0:T(8,128)(2,1)} %broadcast_select_fusion.1), calls=%async_computation | async-start | bytes 262144 | tf_op jit(solution)/shard_map/all_to_all | solution.py:66
  22.4 11.8 %gather_fusion.4 = s32[2048]{0:T(1024)S(1)} fusion(s32[2048]{0:T(1024)S(1)} %bitcast.44, s32[2048]{0:T(1024)S(1)} %fusion.25), kind=kCustom, calls=%fused_computation.clone | custom fusion | bytes 24576 | tf_op jit(solution)/shard_map/jit(_take)/gather | solution.py:76
  34.2 0.7 copy-done.2
  34.9 11.8 %gather_fusion.6 = s32[2048]{0:T(1024)S(1)} fusion(s32[2048]{0:T(1024)S(1)} %copy-done.2, s32[2048]{0:T(1024)S(1)} %broadcast_clamp_fusion), kind=kCustom, calls=%fused_computation.2.clone | custom fusion | bytes 24576 | tf_op jit(solution)/shard_map/jit(_take)/gather | solution.py:80
  46.7 11.8 %gather_fusion.5 = s32[2048]{0:T(1024)S(1)} fusion(s32[2048]{0:T(1024)S(1)} %copy-done.3, s32[2048]{0:T(1024)S(1)} %broadcast_clamp_fusion), kind=kCustom, calls=%fused_computation.1.clone | custom fusion | bytes 24576 | tf_op jit(solution)/shard_map/jit(_take)/gather | solution.py:79
  59.0 0.7 reshape.253
  59.7 8.0 %gather_fusion = bf16[192,128,128]{2,1,0:T(8,128)(2,1)} fusion(bf16[16,128,128]{2,1,0:T(8,128)(2,1)S(1)} %bitcast.45, s32[1024]{0:T(1024)S(1)} %pad_clamp_fusion.2), kind=kCustom, calls=%fused_computation.3 | custom fusion | bytes 12583680 | tf_op jit(solution)/shard_map/jit(_take)/gather | solution.py:69
  67.7 5.8 %all-to-all-start.1 = ((s32[32,1,128]{2,1,0:T(1,128)}), s32[32,1,128]{2,1,0:T(1,128)S(1)}, u32[]{:S(2)}, u32[]{:S(2)}) async-start(s32[32,1,128]{2,1,0:T(1,128)} %reshape.253), calls=%async_computation.1 | async-start | bytes 32768 | tf_op jit(solution)/shard_map/all_to_all | solution.py:83
  73.6 2.2 gather_fusion.2
  75.8 2.4 fusion.9
  78.2 6.6 %fusion.18 = bf16[16,128,128]{1,2,0:T(8,128)(2,1)S(1)} fusion(f32[16,128,128]{1,2,0:T(8,128)S(1)} %fusion.9, bf16[16,12,128,128]{3,2,1,0:T(8,128)(2,1)} %param.15, bf16[16,12,128,128]{3,2,1,0:T(8,128)(2,1)} %bitcast.48, pred[16,12]{1,0:T(8,128)(4,1)S(1)} %compare_and_fusion.2), kind=kOutput, calls=%fused_computation.31 | convolution fusion | flops 808976384 | bytes 14155968 | tf_op jit(solution)/shard_map/ikab,ikbc->iac/dot_general | solution.py:70
  84.7 0.8 copy-done.8
  85.5 1.6 pad_maximum_fusion
  87.1 11.1 %gather_fusion.3 = bf16[2048,512]{1,0:T(8,128)(2,1)} fusion(bf16[2048,512]{1,0:T(8,128)(2,1)} %pad_maximum_fusion, s32[2048]{0:T(1024)S(1)} %broadcast_clamp_fusion), kind=kCustom, calls=%fused_computation.6 | custom fusion | bytes 4202496 | tf_op jit(solution)/shard_map/jit(_take)/gather | solution.py:78
  98.2 2.8 broadcast_select_fusion
  101.0 6.0 %all-to-all-start.2 = ((bf16[32,64,512]{2,1,0:T(8,128)(2,1)}), bf16[32,64,512]{2,1,0:T(8,128)(2,1)}, u32[]{:S(2)}, u32[]{:S(2)}) async-start(bf16[32,64,512]{2,1,0:T(8,128)(2,1)} %broadcast_select_fusion), calls=%async_computation.2 | async-start | bytes 4194304 | tf_op jit(solution)/shard_map/all_to_all | solution.py:82
  107.0 0.7 all-gather.2.cloned.1.call-update
  107.7 73.9 %all_gather.7 = bf16[1024,172]{0,1:T(8,128)(2,1)} all-gather(bf16[256,172]{0,1:T(8,128)(2,1)S(1)} %copy-done.9), channel_id=1, replica_groups=mesh['dom'=8,'rep'=4] {'rep'}, dimensions={0}, use_global_device_ids=true | all-gather | bytes 440320 | tf_op jit(solution)/shard_map/all_gather | solution.py:88
  181.7 0.5 broadcast.150
  182.2 0.7 reduce.14
  183.0 0.6 fusion.32
  184.3 0.8 divide_reduce_fusion
  185.1 0.7 div.54
  185.8 0.6 slice_reduce_fusion
  186.4 0.7 eq.10
  187.1 4.2 %fusion.35 = (f32[1024]{0:T(1024)S(1)}, f32[2048,1024]{1,0:T(8,128)S(1)}) fusion(bf16[2048,512]{1,0:T(8,128)(2,1)} %bitcast.21, bf16[512,1024]{1,0:T(8,128)(2,1)} %all-gather.2.cloned.1.call-done), kind=kOutput, calls=%fused_computation.77 | convolution fusion | flops 2149579776 | bytes 11538432 | tf_op jit(solution)/shard_map/dot_general | solution.py:90
  191.3 0.9 multiply_reduce_fusion.1
  192.2 0.3 copy-done.7
  192.6 1.6 fusion.36
  194.2 1.0 fusion.21
  195.2 0.6 copy-done.13
  195.8 2.5 fusion.23
  198.3 7.4 %fusion = (f32[1024]{0:T(1024)}, f32[1024]{0:T(1024)}, f32[2048,1024]{1,0:T(8,128)}) fusion(f32[2048,1024]{1,0:T(8,128)} %copy-done.4, f32[1024]{0:T(1024)S(1)} %add_rsqrt_fusion, f32[1024]{0:T(1024)S(1)} %broadcast_multiply_fusion.2, bf16[1024,172]{0,1:T(8,128)(2,1)} %all_gather.7, f32[2048,172]{0,1:T(8,128)S(1)} %get-tuple-element.22, f32[2048]{0:T(1024)} %div.54, ...), kind=kOutput, calls=%fused_computation.13 | convolution fusion | flops 738564096 | bytes 18587648 | tf_op jit(solution)/shard_map/dot_general | solution.py:96
  205.8 0.7 broadcast_multiply_fusion
  206.5 10.6 %fusion.4 = f32[512,1024]{1,0:T(8,128)} fusion(bf16[2048,512]{1,0:T(8,128)(2,1)} %bitcast.21, f32[2048,1024]{1,0:T(8,128)} %get-tuple-element.23, f32[2048,1024]{1,0:T(8,128)} %copy-done.4, f32[1024]{0:T(1024)S(1)} %get-tuple-element.24, f32[1024]{0:T(1024)S(1)} %get-tuple-element.25, f32[1024]{0:T(1024)S(1)} %add_rsqrt_fusion, ...), kind=kOutput, calls=%fused_computation.17 | convolution fusion | flops 2166358016 | bytes 20987904 | tf_op jit(solution)/shard_map/dot_general | solution.py:38
  217.2 11.8 %reduce-scatter.8.cloned.1.call-done = f32[256,172]{0,1:T(8,128)} async-done(((f32[1024,172]{0,1:T(8,128)}), f32[256,172]{0,1:T(8,128)}) %reduce-scatter.8.cloned.1.call-update) | async-done | bytes 176144 | tf_op jit(solution)/shard_map/reduce_scatter | solution.py:104
  229.0 44.9 %reduce-scatter.4.cloned.1.call-done = f32[512,256]{1,0:T(8,128)} async-done(((f32[512,1024]{1,0:T(8,128)}), f32[512,256]{1,0:T(8,128)}) %reduce-scatter.4.cloned.1.call-update) | async-done | bytes 524304 | tf_op jit(solution)/shard_map/reduce_scatter | solution.py:103
  274.1 0.1 multiply_reduce_fusion.2
  274.2 0.5 fusion.26
  274.7 54.4 %all-reduce.2.cloned.1.call-done = f32[256,172]{0,1:T(8,128)} async-done(((f32[256,172]{0,1:T(8,128)}), f32[256,172]{0,1:T(8,128)}) %all-reduce.2.cloned.1.call-update) | async-done | bytes 176144 | tf_op jit(solution)/shard_map/psum | solution.py:107
  329.2 37.7 %reduce-scatter.6.cloned.1.call-done = f32[64,256]{1,0:T(8,128)} async-done(((f32[512,256]{1,0:T(8,128)}), f32[64,256]{1,0:T(8,128)}) %reduce-scatter.6.cloned.1.call-update) | async-done | bytes 65552 | tf_op jit(solution)/shard_map/reduce_scatter | solution.py:106
  366.9 1.6 copy.25
  (75 shorter events, 1.3 us)
Async XLA Ops:
  7.2 68.6 %copy-start = (bf16[16,4,128,128]{3,2,1,0:T(8,128)(2,1)S(1)}, bf16[16,4,128,128]{3,2,1,0:T(8,128)(2,1)}, u32[]{:S(2)}) copy-start(bf16[16,4,128,128]{3,2,1,0:T(8,128)(2,1)} %param.17) | copy-start | bytes 6291460
  10.0 12.1 %copy-start.18 = (s32[16,4]{0,1:T(4,128)S(1)}, s32[16,4]{0,1:T(4,128)}, u32[]{:S(2)}) copy-start(s32[16,4]{0,1:T(4,128)} %param.18) | copy-start | bytes 772
  10.0 12.4 %copy-start.10 = (s32[1,2048]{1,0:T(1,128)S(1)}, s32[1,2048]{1,0:T(1,128)}, u32[]{:S(2)}) copy-start(s32[1,2048]{1,0:T(1,128)} %param.21) | copy-start | bytes 24580
  10.0 12.4 %copy-start.1 = (s32[1,2048]{1,0:T(1,128)S(1)}, s32[1,2048]{1,0:T(1,128)}, u32[]{:S(2)}) copy-start(s32[1,2048]{1,0:T(1,128)} %param.20) | copy-start | bytes 24580
  14.8 53.0 %all-to-all-start = ((bf16[32,16,128]{2,1,0:T(8,128)(2,1)}), bf16[32,16,128]{2,1,0:T(8,128)(2,1)S(1)}, u32[]{:S(2)}, u32[]{:S(2)}) async-start(bf16[32,16,128]{2,1,0:T(8,128)(2,1)} %broadcast_select_fusion.1), calls=%async_computation | async-start | bytes 262144 | tf_op jit(solution)/shard_map/all_to_all | solution.py:66
  34.2 0.7 copy-start.2
  34.9 11.8 %copy-start.3 = (s32[2048]{0:T(1024)S(1)}, s32[2048]{0:T(1024)}, u32[]{:S(2)}) copy-start(s32[2048]{0:T(1024)} %param.22) | copy-start | bytes 24580
  46.7 12.0 %copy-start.16 = (s32[16,12]{1,0:T(8,128)S(1)}, s32[16,12]{1,0:T(8,128)}, u32[]{:S(2)}) copy-start(s32[16,12]{1,0:T(8,128)} %param.16) | copy-start | bytes 2308
  67.7 33.2 %all-to-all-start.1 = ((s32[32,1,128]{2,1,0:T(1,128)}), s32[32,1,128]{2,1,0:T(1,128)S(1)}, u32[]{:S(2)}, u32[]{:S(2)}) async-start(s32[32,1,128]{2,1,0:T(1,128)} %reshape.253), calls=%async_computation.1 | async-start | bytes 32768 | tf_op jit(solution)/shard_map/all_to_all | solution.py:83
  78.1 7.4 %copy-start.5 = (bf16[2048,128]{1,0:T(8,128)(2,1)S(1)}, bf16[2048,128]{1,0:T(8,128)(2,1)}, u32[]{:S(2)}) copy-start(bf16[2048,128]{1,0:T(8,128)(2,1)} %get-tuple-element.13) | copy-start | bytes 1572868
  78.1 7.4 %copy-start.6 = (bf16[2048,128]{1,0:T(8,128)(2,1)S(1)}, bf16[2048,128]{1,0:T(8,128)(2,1)}, u32[]{:S(2)}) copy-start(bf16[2048,128]{1,0:T(8,128)(2,1)} %get-tuple-element.16) | copy-start | bytes 1572868
  84.7 0.8 copy-start.8
  101.0 6.8 %copy-start.9 = (bf16[256,172]{0,1:T(8,128)(2,1)S(1)}, bf16[256,172]{0,1:T(8,128)(2,1)}, u32[]{:S(2)}) copy-start(bf16[256,172]{0,1:T(8,128)(2,1)} %param.25) | copy-start | bytes 264196
  101.0 86.1 %all-to-all-start.2 = ((bf16[32,64,512]{2,1,0:T(8,128)(2,1)}), bf16[32,64,512]{2,1,0:T(8,128)(2,1)}, u32[]{:S(2)}, u32[]{:S(2)}) async-start(bf16[32,64,512]{2,1,0:T(8,128)(2,1)} %broadcast_select_fusion), calls=%async_computation.2 | async-start | bytes 4194304 | tf_op jit(solution)/shard_map/all_to_all | solution.py:82
  107.0 80.1 %all-gather.2.cloned.1.call-start = ((), (), s32[]{:S(2)}) async-start(), calls=%async_computation.6 | async-start | bytes 1310720 | tf_op jit(solution)/shard_map/all_gather | solution.py:87
  107.7 121.3 %reduce-scatter.8.cloned.1.call-start = ((), (), s32[]{:S(2)}) async-start(), calls=%async_computation.9 | async-start | bytes 901120 | tf_op jit(solution)/shard_map/reduce_scatter | solution.py:104
  191.3 3.9 %copy-start.4 = (f32[2048,1024]{1,0:T(8,128)}, f32[2048,1024]{1,0:T(8,128)S(1)}, u32[]{:S(2)}) copy-start(f32[2048,1024]{1,0:T(8,128)S(1)} %get-tuple-element.20) | copy-start | bytes 25165828
  191.3 1.3 copy-start.7
  192.6 1.6 copy-start.12
  192.6 3.2 copy-start.17
  195.2 0.6 copy-start.13
  205.7 68.2 %reduce-scatter.4.cloned.1.call-start = ((), (), s32[]{:S(2)}) async-start(), calls=%async_computation.7 | async-start | bytes 2621440 | tf_op jit(solution)/shard_map/reduce_scatter | solution.py:103
  217.1 56.9 %copy-start.14 = (f32[2048]{0:T(1024)S(1)}, f32[2048]{0:T(1024)}, u32[]{:S(2)}) copy-start(f32[2048]{0:T(1024)} %copy-done.13) | copy-start | bytes 24580
  217.1 56.9 %copy-start.15 = (f32[2048]{0:T(1024)S(1)}, f32[2048]{0:T(1024)}, u32[]{:S(2)}) copy-start(f32[2048]{0:T(1024)} %get-tuple-element.8) | copy-start | bytes 24580
  217.1 57.0 %copy-start.11 = (f32[1,32,64]{2,0,1:T(1,128)S(1)}, f32[1,32,64]{2,0,1:T(1,128)}, u32[]{:S(2)}) copy-start(f32[1,32,64]{2,0,1:T(1,128)} %get-tuple-element.18) | copy-start | bytes 24580
  217.1 57.1 %copy-start.19 = (f32[32]{0:T(128)S(1)}, f32[32]{0:T(128)}, u32[]{:S(2)}) copy-start(f32[32]{0:T(128)} %get-tuple-element.10) | copy-start | bytes 388
  217.1 112.0 %all-reduce.2.cloned.1.call-start = ((), (), s32[]{:S(2)}) async-start(), calls=%async_computation.10 | async-start | bytes 360448 | tf_op jit(solution)/shard_map/psum | solution.py:107
  229.0 137.9 %reduce-scatter.6.cloned.1.call-start = ((), (), s32[]{:S(2)}) async-start(), calls=%async_computation.8 | async-start | bytes 589824 | tf_op jit(solution)/shard_map/reduce_scatter | solution.py:106
Sparse Core Ops, SparseCore 0:
  109.3 55.8 all-gather.1
  205.8 23.0 reduce-scatter.7
  231.2 42.6 reduce-scatter.3
  276.9 52.1 all-reduce.1
  332.6 34.2 reduce-scatter.5
where the time goes:
time: 376 us; the launch traced here: 375 us
  waiting for transfers between devices  150 us (40%)
  blocking collectives  73.9 us (20%)
  local copies, waits for them, and re-layouts  68.5 us (18%)
  matrix products  35.3 us (9%)
  starting transfers between devices  19.3 us (5%)
  between operations  14.8 us (4%)
  other arithmetic  13.5 us (4%)
    all_gather x1, blocking collectives, shards(): lax.all_gather(w_second, 'rep', axis=0, tiled=True)  73.9 us
    psum x1, waiting for transfers between devices, shards(): grad_two = lax.psum(grad_two_rep, 'dom')  54.4 us
    reduce_scatter x1, waiting for transfers between devices, shards(): lax.psum_scatter(grad_one_full, 'rep', scatter_dimension=1, tiled=True)  44.9 us
    reduce_scatter x1, waiting for transfers between devices, shards(): lax.psum_scatter(grad_one_rep, 'dom', scatter_dimension=0, tiled=True)  37.7 us
    dot_general x2, matrix products, contract_rows(): lax.dot_general(left, right, (((0,), (0,)), ((), ())), preferred_element_...  13.2 us
    gather x1, local copies, waits for them, and re-layouts, shards(): order = jnp.take(train_ids[0], shuffle[0], axis=0)  11.8 us
    gather x1, local copies, waits for them, and re-layouts, shards(): own_labels = jnp.take(labels, order, axis=0)  11.8 us
    gather x1, local copies, waits for them, and re-layouts, shards(): own_marks = jnp.take(labelled, order, axis=0)  11.8 us
  transfers between devices with their start and end apart: 8, of which 4 were waited for; matrix products, arithmetic and copies ran while one was open for 23% of the time, Pallas kernels for 0%

commit v1 on v0

--- a/solution.py
+++ b/solution.py
@@ -104,7 +104,7 @@
         lax.psum_scatter(grad_two_full, "rep", scatter_dimension=0, tiled=True),
     )
     grad_one = lax.psum_scatter(grad_one_rep, "dom", scatter_dimension=0, tiled=True)
-    grad_two = lax.psum(grad_two_rep, "dom")
+    grad_two = jnp.sum(lax.all_gather(grad_two_rep, "dom"), axis=0)
     loss = source_losses(cross, weights_row, devices)
     return (next_hop, loss.reshape(1, devices), grad_one, grad_two)
 

time: 376 us -> 345 us (0.918)
  waiting for transfers between devices: 150 us -> 118 us
    psum x1 -> x0, waiting for transfers between devices: 54.4 us -> none  [shards(): grad_two = lax.psum(grad_two_rep, 'dom')]
    all_gather x0 -> x1, waiting for transfers between devices: none -> 25.4 us  [shards(): grad_two = jnp.sum(lax.all_gather(grad_two_rep, 'dom'), axis=0)]
  transfers between devices with their start and end apart: 8 -> 8, of which waited for: 4 -> 4; matrix products, arithmetic and copies ran while one was open for 23% -> 26% of each run, Pallas kernels for 0% -> 0%
where the time goes in v1:
time: 345 us; the launch traced here: 344 us
  waiting for transfers between devices  118 us (34%)
  blocking collectives  73.9 us (21%)
  local copies, waits for them, and re-layouts  68.8 us (20%)
  matrix products  35.3 us (10%)
  starting transfers between devices  19.3 us (6%)
  between operations  14.8 us (4%)
  other arithmetic  14.5 us (4%)
    all_gather x1, blocking collectives, shards(): lax.all_gather(w_second, 'rep', axis=0, tiled=True)  73.9 us
    reduce_scatter x1, waiting for transfers between devices, shards(): lax.psum_scatter(grad_one_full, 'rep', scatter_dimension=1, tiled=True)  44.9 us
    reduce_scatter x1, waiting for transfers between devices, shards(): lax.psum_scatter(grad_one_rep, 'dom', scatter_dimension=0, tiled=True)  34.7 us
    all_gather x1, waiting for transfers between devices, shards(): grad_two = jnp.sum(lax.all_gather(grad_two_rep, 'dom'), axis=0)  25.4 us
    dot_general x2, matrix products, contract_rows(): lax.dot_general(left, right, (((0,), (0,)), ((), ())), preferred_element_...  13.2 us
    gather x1, local copies, waits for them, and re-layouts, shards(): order = jnp.take(train_ids[0], shuffle[0], axis=0)  11.8 us
    gather x1, local copies, waits for them, and re-layouts, shards(): own_labels = jnp.take(labels, order, axis=0)  11.8 us
    gather x1, local copies, waits for them, and re-layouts, shards(): own_marks = jnp.take(labelled, order, axis=0)  11.8 us
  transfers between devices with their start and end apart: 8, of which 4 were waited for; matrix products, arithmetic and copies ran while one was open for 26% of the time, Pallas kernels for 0%

profile of v1, /device:TPU:0, one launch (start us, length us, event | category | flops | bytes accessed | tf_op | source)
XLA Modules:
  0.0 344.3 jit_solution(5102519077817672114)
XLA Ops:
  7.2 0.8 compare_select_fusion.5
  8.0 0.5 broadcast.147
  8.5 1.3 reduce.13
  10.0 2.6 slice_bitcast_fusion.1
  12.7 1.3 gather_fusion.1
  14.0 0.8 broadcast_select_fusion.1
  14.8 7.3 %all-to-all-start = ((bf16[32,16,128]{2,1,0:T(8,128)(2,1)}), bf16[32,16,128]{2,1,0:T(8,128)(2,1)S(1)}, u32[]{:S(2)}, u32[]{:S(2)}) async-start(bf16[32,16,128]{2,1,0:T(8,128)(2,1)} %broadcast_select_fusion.1), calls=%async_computation | async-start | bytes 262144 | tf_op jit(solution)/shard_map/all_to_all | solution.py:66
  22.4 11.8 %gather_fusion.4 = s32[2048]{0:T(1024)S(1)} fusion(s32[2048]{0:T(1024)S(1)} %bitcast.50, s32[2048]{0:T(1024)S(1)} %fusion.25), kind=kCustom, calls=%fused_computation.clone | custom fusion | bytes 24576 | tf_op jit(solution)/shard_map/jit(_take)/gather | solution.py:76
  34.2 0.7 copy-done.2
  34.9 11.8 %gather_fusion.6 = s32[2048]{0:T(1024)S(1)} fusion(s32[2048]{0:T(1024)S(1)} %copy-done.2, s32[2048]{0:T(1024)S(1)} %broadcast_clamp_fusion), kind=kCustom, calls=%fused_computation.2.clone | custom fusion | bytes 24576 | tf_op jit(solution)/shard_map/jit(_take)/gather | solution.py:80
  46.7 11.8 %gather_fusion.5 = s32[2048]{0:T(1024)S(1)} fusion(s32[2048]{0:T(1024)S(1)} %copy-done.3, s32[2048]{0:T(1024)S(1)} %broadcast_clamp_fusion), kind=kCustom, calls=%fused_computation.1.clone | custom fusion | bytes 24576 | tf_op jit(solution)/shard_map/jit(_take)/gather | solution.py:79
  59.0 0.7 reshape.254
  59.7 8.0 %gather_fusion = bf16[192,128,128]{2,1,0:T(8,128)(2,1)} fusion(bf16[16,128,128]{2,1,0:T(8,128)(2,1)S(1)} %bitcast.51, s32[1024]{0:T(1024)S(1)} %pad_clamp_fusion.2), kind=kCustom, calls=%fused_computation.3 | custom fusion | bytes 12583680 | tf_op jit(solution)/shard_map/jit(_take)/gather | solution.py:69
  67.7 5.8 %all-to-all-start.1 = ((s32[32,1,128]{2,1,0:T(1,128)}), s32[32,1,128]{2,1,0:T(1,128)S(1)}, u32[]{:S(2)}, u32[]{:S(2)}) async-start(s32[32,1,128]{2,1,0:T(1,128)} %reshape.254), calls=%async_computation.1 | async-start | bytes 32768 | tf_op jit(solution)/shard_map/all_to_all | solution.py:83
  73.6 2.2 gather_fusion.2
  75.8 2.4 fusion.9
  78.2 6.6 %fusion.18 = bf16[16,128,128]{1,2,0:T(8,128)(2,1)S(1)} fusion(f32[16,128,128]{1,2,0:T(8,128)S(1)} %fusion.9, bf16[16,12,128,128]{3,2,1,0:T(8,128)(2,1)} %param.15, bf16[16,12,128,128]{3,2,1,0:T(8,128)(2,1)} %bitcast.54, pred[16,12]{1,0:T(8,128)(4,1)S(1)} %compare_and_fusion.2), kind=kOutput, calls=%fused_computation.32 | convolution fusion | flops 808976384 | bytes 14155968 | tf_op jit(solution)/shard_map/ikab,ikbc->iac/dot_general | solution.py:70
  84.7 0.8 copy-done.8
  85.5 1.6 pad_maximum_fusion
  87.1 11.1 %gather_fusion.3 = bf16[2048,512]{1,0:T(8,128)(2,1)} fusion(bf16[2048,512]{1,0:T(8,128)(2,1)} %pad_maximum_fusion, s32[2048]{0:T(1024)S(1)} %broadcast_clamp_fusion), kind=kCustom, calls=%fused_computation.6 | custom fusion | bytes 4202496 | tf_op jit(solution)/shard_map/jit(_take)/gather | solution.py:78
  98.2 2.8 broadcast_select_fusion
  101.0 6.0 %all-to-all-start.2 = ((bf16[32,64,512]{2,1,0:T(8,128)(2,1)}), bf16[32,64,512]{2,1,0:T(8,128)(2,1)}, u32[]{:S(2)}, u32[]{:S(2)}) async-start(bf16[32,64,512]{2,1,0:T(8,128)(2,1)} %broadcast_select_fusion), calls=%async_computation.2 | async-start | bytes 4194304 | tf_op jit(solution)/shard_map/all_to_all | solution.py:82
  107.0 0.7 all-gather.4.cloned.1.call-update
  107.7 73.9 %all_gather.13 = bf16[1024,172]{0,1:T(8,128)(2,1)} all-gather(bf16[256,172]{0,1:T(8,128)(2,1)S(1)} %copy-done.9), channel_id=1, replica_groups=mesh['dom'=8,'rep'=4] {'rep'}, dimensions={0}, use_global_device_ids=true | all-gather | bytes 440320 | tf_op jit(solution)/shard_map/all_gather | solution.py:88
  181.7 0.5 broadcast.150
  182.2 0.7 reduce.14
  183.0 0.6 fusion.32
  184.3 0.8 divide_reduce_fusion
  185.1 0.7 div.54
  185.8 0.6 slice_reduce_fusion
  186.4 0.7 eq.10
  187.1 4.2 %fusion.35 = (f32[1024]{0:T(1024)S(1)}, f32[2048,1024]{1,0:T(8,128)S(1)}) fusion(bf16[2048,512]{1,0:T(8,128)(2,1)} %bitcast.21, bf16[512,1024]{1,0:T(8,128)(2,1)} %all-gather.4.cloned.1.call-done), kind=kOutput, calls=%fused_computation.78 | convolution fusion | flops 2149579776 | bytes 11538432 | tf_op jit(solution)/shard_map/dot_general | solution.py:90
  191.3 0.9 multiply_reduce_fusion.1
  192.2 0.3 copy-done.7
  192.6 1.6 fusion.36
  194.2 1.0 fusion.21
  195.2 0.6 copy-done.13
  195.8 2.5 fusion.23
  198.3 7.4 %fusion = (f32[1024]{0:T(1024)}, f32[1024]{0:T(1024)}, f32[2048,1024]{1,0:T(8,128)}) fusion(f32[2048,1024]{1,0:T(8,128)} %copy-done.4, f32[1024]{0:T(1024)S(1)} %add_rsqrt_fusion, f32[1024]{0:T(1024)S(1)} %broadcast_multiply_fusion.2, bf16[1024,172]{0,1:T(8,128)(2,1)} %all_gather.13, f32[2048,172]{0,1:T(8,128)S(1)} %get-tuple-element.22, f32[2048]{0:T(1024)} %div.54, ...), kind=kOutput, calls=%fused_computation.13 | convolution fusion | flops 738564096 | bytes 18587648 | tf_op jit(solution)/shard_map/dot_general | solution.py:96
  205.8 0.7 broadcast_multiply_fusion
  206.5 10.6 %fusion.4 = f32[512,1024]{1,0:T(8,128)} fusion(bf16[2048,512]{1,0:T(8,128)(2,1)} %bitcast.21, f32[2048,1024]{1,0:T(8,128)} %get-tuple-element.23, f32[2048,1024]{1,0:T(8,128)} %copy-done.4, f32[1024]{0:T(1024)S(1)} %get-tuple-element.24, f32[1024]{0:T(1024)S(1)} %get-tuple-element.25, f32[1024]{0:T(1024)S(1)} %add_rsqrt_fusion, ...), kind=kOutput, calls=%fused_computation.17 | convolution fusion | flops 2166358016 | bytes 20987904 | tf_op jit(solution)/shard_map/dot_general | solution.py:38
  217.2 11.8 %reduce-scatter.8.cloned.1.call-done = f32[256,172]{0,1:T(8,128)} async-done(((f32[1024,172]{0,1:T(8,128)}), f32[256,172]{0,1:T(8,128)}) %reduce-scatter.8.cloned.1.call-update) | async-done | bytes 176144 | tf_op jit(solution)/shard_map/reduce_scatter | solution.py:104
  229.0 44.9 %reduce-scatter.4.cloned.1.call-done = f32[512,256]{1,0:T(8,128)} async-done(((f32[512,1024]{1,0:T(8,128)}), f32[512,256]{1,0:T(8,128)}) %reduce-scatter.4.cloned.1.call-update) | async-done | bytes 524304 | tf_op jit(solution)/shard_map/reduce_scatter | solution.py:103
  274.2 0.5 fusion.26
  274.7 25.4 %all-gather.6.cloned.1.call-done = f32[2048,172]{0,1:T(8,128)} async-done(((f32[256,172]{0,1:T(8,128)}), f32[2048,172]{0,1:T(8,128)}) %all-gather.6.cloned.1.call-update) | async-done | bytes 1409040 | tf_op jit(solution)/shard_map/all_gather | solution.py:107
  300.1 1.9 copy.24
  302.0 1.0 bitcast_reduce_fusion
  303.1 34.7 %reduce-scatter.6.cloned.1.call-done = f32[64,256]{1,0:T(8,128)} async-done(((f32[512,256]{1,0:T(8,128)}), f32[64,256]{1,0:T(8,128)}) %reduce-scatter.6.cloned.1.call-update) | async-done | bytes 65552 | tf_op jit(solution)/shard_map/reduce_scatter | solution.py:106
  (76 shorter events, 1.4 us)
Async XLA Ops:
  7.2 68.6 %copy-start = (bf16[16,4,128,128]{3,2,1,0:T(8,128)(2,1)S(1)}, bf16[16,4,128,128]{3,2,1,0:T(8,128)(2,1)}, u32[]{:S(2)}) copy-start(bf16[16,4,128,128]{3,2,1,0:T(8,128)(2,1)} %param.17) | copy-start | bytes 6291460
  10.0 12.1 %copy-start.18 = (s32[16,4]{0,1:T(4,128)S(1)}, s32[16,4]{0,1:T(4,128)}, u32[]{:S(2)}) copy-start(s32[16,4]{0,1:T(4,128)} %param.18) | copy-start | bytes 772
  10.0 12.4 %copy-start.10 = (s32[1,2048]{1,0:T(1,128)S(1)}, s32[1,2048]{1,0:T(1,128)}, u32[]{:S(2)}) copy-start(s32[1,2048]{1,0:T(1,128)} %param.21) | copy-start | bytes 24580
  10.0 12.4 %copy-start.1 = (s32[1,2048]{1,0:T(1,128)S(1)}, s32[1,2048]{1,0:T(1,128)}, u32[]{:S(2)}) copy-start(s32[1,2048]{1,0:T(1,128)} %param.20) | copy-start | bytes 24580
  14.8 53.0 %all-to-all-start = ((bf16[32,16,128]{2,1,0:T(8,128)(2,1)}), bf16[32,16,128]{2,1,0:T(8,128)(2,1)S(1)}, u32[]{:S(2)}, u32[]{:S(2)}) async-start(bf16[32,16,128]{2,1,0:T(8,128)(2,1)} %broadcast_select_fusion.1), calls=%async_computation | async-start | bytes 262144 | tf_op jit(solution)/shard_map/all_to_all | solution.py:66
  34.2 0.7 copy-start.2
  34.9 11.8 %copy-start.3 = (s32[2048]{0:T(1024)S(1)}, s32[2048]{0:T(1024)}, u32[]{:S(2)}) copy-start(s32[2048]{0:T(1024)} %param.22) | copy-start | bytes 24580
  46.7 12.0 %copy-start.16 = (s32[16,12]{1,0:T(8,128)S(1)}, s32[16,12]{1,0:T(8,128)}, u32[]{:S(2)}) copy-start(s32[16,12]{1,0:T(8,128)} %param.16) | copy-start | bytes 2308
  67.7 33.2 %all-to-all-start.1 = ((s32[32,1,128]{2,1,0:T(1,128)}), s32[32,1,128]{2,1,0:T(1,128)S(1)}, u32[]{:S(2)}, u32[]{:S(2)}) async-start(s32[32,1,128]{2,1,0:T(1,128)} %reshape.254), calls=%async_computation.1 | async-start | bytes 32768 | tf_op jit(solution)/shard_map/all_to_all | solution.py:83
  78.1 7.4 %copy-start.5 = (bf16[2048,128]{1,0:T(8,128)(2,1)S(1)}, bf16[2048,128]{1,0:T(8,128)(2,1)}, u32[]{:S(2)}) copy-start(bf16[2048,128]{1,0:T(8,128)(2,1)} %get-tuple-element.13) | copy-start | bytes 1572868
  78.1 7.4 %copy-start.6 = (bf16[2048,128]{1,0:T(8,128)(2,1)S(1)}, bf16[2048,128]{1,0:T(8,128)(2,1)}, u32[]{:S(2)}) copy-start(bf16[2048,128]{1,0:T(8,128)(2,1)} %get-tuple-element.16) | copy-start | bytes 1572868
  84.7 0.8 copy-start.8
  101.0 6.8 %copy-start.9 = (bf16[256,172]{0,1:T(8,128)(2,1)S(1)}, bf16[256,172]{0,1:T(8,128)(2,1)}, u32[]{:S(2)}) copy-start(bf16[256,172]{0,1:T(8,128)(2,1)} %param.25) | copy-start | bytes 264196
  101.0 86.1 %all-to-all-start.2 = ((bf16[32,64,512]{2,1,0:T(8,128)(2,1)}), bf16[32,64,512]{2,1,0:T(8,128)(2,1)}, u32[]{:S(2)}, u32[]{:S(2)}) async-start(bf16[32,64,512]{2,1,0:T(8,128)(2,1)} %broadcast_select_fusion), calls=%async_computation.2 | async-start | bytes 4194304 | tf_op jit(solution)/shard_map/all_to_all | solution.py:82
  107.0 80.1 %all-gather.4.cloned.1.call-start = ((), (), s32[]{:S(2)}) async-start(), calls=%async_computation.6 | async-start | bytes 1310720 | tf_op jit(solution)/shard_map/all_gather | solution.py:87
  107.7 121.3 %reduce-scatter.8.cloned.1.call-start = ((), (), s32[]{:S(2)}) async-start(), calls=%async_computation.9 | async-start | bytes 901120 | tf_op jit(solution)/shard_map/reduce_scatter | solution.py:104
  191.3 3.9 %copy-start.4 = (f32[2048,1024]{1,0:T(8,128)}, f32[2048,1024]{1,0:T(8,128)S(1)}, u32[]{:S(2)}) copy-start(f32[2048,1024]{1,0:T(8,128)S(1)} %get-tuple-element.20) | copy-start | bytes 25165828
  191.3 1.3 copy-start.7
  192.6 1.6 copy-start.12
  192.6 3.2 copy-start.17
  195.2 0.6 copy-start.13
  205.7 68.2 %reduce-scatter.4.cloned.1.call-start = ((), (), s32[]{:S(2)}) async-start(), calls=%async_computation.7 | async-start | bytes 2621440 | tf_op jit(solution)/shard_map/reduce_scatter | solution.py:103
  217.1 56.9 %copy-start.14 = (f32[2048]{0:T(1024)S(1)}, f32[2048]{0:T(1024)}, u32[]{:S(2)}) copy-start(f32[2048]{0:T(1024)} %copy-done.13) | copy-start | bytes 24580
  217.1 56.9 %copy-start.15 = (f32[2048]{0:T(1024)S(1)}, f32[2048]{0:T(1024)}, u32[]{:S(2)}) copy-start(f32[2048]{0:T(1024)} %get-tuple-element.8) | copy-start | bytes 24580
  217.1 57.0 %copy-start.11 = (f32[1,32,64]{2,0,1:T(1,128)S(1)}, f32[1,32,64]{2,0,1:T(1,128)}, u32[]{:S(2)}) copy-start(f32[1,32,64]{2,0,1:T(1,128)} %get-tuple-element.18) | copy-start | bytes 24580
  217.1 57.1 %copy-start.19 = (f32[32]{0:T(128)S(1)}, f32[32]{0:T(128)}, u32[]{:S(2)}) copy-start(f32[32]{0:T(128)} %get-tuple-element.10) | copy-start | bytes 388
  217.1 83.0 %all-gather.6.cloned.1.call-start = ((), (), s32[]{:S(2)}) async-start(), calls=%async_computation.10 | async-start | bytes 1622016 | tf_op jit(solution)/shard_map/all_gather | solution.py:107
  229.0 108.8 %reduce-scatter.6.cloned.1.call-start = ((), (), s32[]{:S(2)}) async-start(), calls=%async_computation.8 | async-start | bytes 589824 | tf_op jit(solution)/shard_map/reduce_scatter | solution.py:106
Sparse Core Ops, SparseCore 0:
  109.3 55.8 all-gather.3
  205.8 23.0 reduce-scatter.7
  231.2 42.6 reduce-scatter.3
  275.7 24.4 all-gather.5
  303.6 34.1 reduce-scatter.5
